TPU v7x, 128 devices: a whole 4x4x4 slice. The times are simulated.
128 devices in a mesh: row: 16 (over z, y), col: 8 (over x, core).
Axes of the slice: x: 4, y: 4, z: 4, core: 2. Of those that a mesh axis runs over, the one named last changes fastest.
Arguments:
- trailing: float32 [16384, 16384], P('row', 'col'), may hold values from -40 to 40, as said below
- factor_one: float32 [16384, 512], P(('row', 'col')), may hold values from -0.0390625 to 0.0390625
- inverse_one: float32 [512, 512], replicated, may hold values from -1 to 2, as said below
- factor_two_top: float32 [512, 512], replicated, may hold values from -0.0390625 to 0.0390625
- factor_two: float32 [16384, 512], P(('row', 'col')), may hold values from -0.0390625 to 0.0390625
- inverse_two: float32 [512, 512], replicated, may hold values from -1 to 2, as said below
- structure_one: int32 [96], replicated, may hold values from 0 to 127, as said below
- structure_two: int32 [94], replicated, may hold values from 0 to 127, as said below
Outputs:
- column_one: float32 [16384, 512], P(('row', 'col'))
- diagonal_one: float32 [512, 512], replicated
- column_two: float32 [16384, 512], P(('row', 'col'))
- cross_two: float32 [512, 512], replicated
- diagonal_two: float32 [512, 512], replicated
Inputs may be any that keep to these rules, and one draw needn't show every extreme that they name: `trailing`: symmetric. `inverse_one`: lower triangular, diagonal between 1 and 2. `inverse_two`: lower triangular, diagonal between 1 and 2. `structure_one`: distinct, rising; lists block 0 and the last block. `structure_two`: distinct, rising, each also listed in structure_one; lists block 0 and the last block.
All inputs are finite; a program needn't handle non-finite values.
Results may differ from a plain program's by a relative error of at most 0.0003.
Values sent between devices are 32-bit elements; how exact they have to be, the bound alone decides.
No kernel may reach another device: no remote copies, remote signals or barrier semaphores. Data moves between devices by JAX's collectives and lax.ppermute only.
A program may use at most 128 MiB of HBM per device.

v0:
```python
import jax
import jax.numpy as jnp
from jax import lax
from jax.sharding import PartitionSpec as P

BLK = 128


def spread(x, axis, root):
    mine = lax.axis_index(axis) == root
    return lax.psum(jnp.where(mine, x, jnp.zeros_like(x)), axis)


def product(left, right):
    return jnp.dot(left, right, precision=lax.Precision.HIGHEST, preferred_element_type=jnp.float32)


def block_flags(structure, first_row, count):
    blocks = (first_row + jnp.arange(count, dtype=jnp.int32)) // BLK
    hits = jnp.any(blocks[:, None] == structure[None, :], axis=1)
    return hits.astype(jnp.float32)[:, None]


def panel_apart(normal, col_index, spread_count):
    row_block = lax.all_gather(normal, "col", axis=0, tiled=True)
    pieces = []
    for offset in range(spread_count):
        pieces.append(spread(row_block, "row", col_index * spread_count + offset))
    return (row_block, jnp.concatenate(pieces, axis=0))


def sweep(trailing, col_block, own_normal):
    summed = lax.psum_scatter(-product(trailing, col_block), "col", scatter_dimension=0, tiled=True)
    quad_part = product(own_normal.T, summed)
    return (summed, quad_part)


def body(
    trailing,
    factor_one,
    inverse_one,
    factor_two_top,
    factor_two,
    inverse_two,
    structure_one,
    structure_two,
):
    piece_rows = factor_one.shape[0]
    spread_count = lax.axis_size("row") // lax.axis_size("col")
    row_index = lax.axis_index("row")
    col_index = lax.axis_index("col")
    first_row = (row_index * lax.axis_size("col") + col_index) * piece_rows
    mask_one = block_flags(structure_one, first_row, piece_rows)
    mask_two = block_flags(structure_two, first_row, piece_rows)
    normal_one = mask_one * product(factor_one, inverse_one)
    normal_two = mask_two * product(factor_two, inverse_two)
    rows_one, cols_one = panel_apart(normal_one, col_index, spread_count)
    rows_two, cols_two = panel_apart(normal_two, col_index, spread_count)
    summed_one, quad_one = sweep(trailing, cols_one, normal_one)
    column_one = mask_one * summed_one
    diag_total = lax.psum(quad_one, ("row", "col"))
    diagonal_one = product(inverse_one.T, inverse_one) - diag_total
    normal_top = product(factor_two_top, inverse_two)
    summed_two, quad_two = sweep(trailing, cols_two, normal_two)
    local_part = -product(column_one, normal_top)
    column_two = mask_two * (local_part + summed_two)
    cross_total, second_total = lax.psum(
        (product(column_one.T, normal_two), product(normal_two.T, local_part) + quad_two),
        ("row", "col"),
    )
    cross_two = -(product(diagonal_one, normal_top) + cross_total)
    diagonal_two = (
        product(inverse_two.T, inverse_two) - product(normal_top.T, cross_two) - second_total
    )
    return (column_one, diagonal_one, column_two, cross_two, diagonal_two)


def solution(mesh):
    return jax.shard_map(
        body,
        mesh=mesh,
        in_specs=(
            P("row", "col"),
            P(("row", "col"), None),
            P(),
            P(),
            P(("row", "col"), None),
            P(),
            P(),
            P(),
        ),
        out_specs=(P(("row", "col"), None), P(), P(("row", "col"), None), P(), P()),
        check_vma=False,
    )
```

profile of v0, /device:TPU:1, one launch (start us, length us, event | category | flops | bytes accessed | tf_op | source)
XLA Modules:
  0.0 474.7 jit_solution(2318638378639296707)
XLA Ops:
  7.2 0.0 copy-start
  7.2 0.0 copy-start.1
  7.2 0.0 all-gather.5.cloned.1.call-start
  7.3 0.9 compare_reduce_fusion
  8.2 0.3 copy-done
  8.4 2.4 convolution_multiply_fusion
  10.8 0.0 all-gather.5.cloned.1.call-update
  10.8 0.0 all-gather.3.cloned.1.call-start
  10.9 0.7 compare_reduce_fusion.1
  11.6 0.0 copy-done.1
  11.6 2.4 convolution_multiply_fusion.1
  14.0 0.0 all-gather.3.cloned.1.call-update
  14.0 0.0 all-reduce.7.cloned.1.call-start
  14.1 25.6 %all-gather.5.cloned.1.call-done = f32[1024,512]{1,0:T(8,128)} async-done(((f32[128,512]{1,0:T(8,128)}), f32[1024,512]{1,0:T(8,128)}) %all-gather.5.cloned.1.call-update) | async-done | bytes 2097168 | tf_op jit(solution)/shard_map/all_gather | solution.py:25
  39.7 4.2 broadcast_select_fusion.1
  43.9 23.5 %all-gather.3.cloned.1.call-done = f32[1024,512]{1,0:T(8,128)} async-done(((f32[128,512]{1,0:T(8,128)}), f32[1024,512]{1,0:T(8,128)}) %all-gather.3.cloned.1.call-update) | async-done | bytes 2097168 | tf_op jit(solution)/shard_map/all_gather | solution.py:25
  67.5 4.2 broadcast_select_fusion.3
  71.6 0.0 all-reduce.7.cloned.1.call-update
  71.7 0.0 reduce-scatter.3.cloned.1.call-start
  71.7 142.3 %all-reduce.7.cloned.1.call-done = (f32[1024,512]{1,0:T(8,128)}, f32[1024,512]{1,0:T(8,128)}, f32[1024,512]{1,0:T(8,128)}, f32[1024,512]{1,0:T(8,128)}) async-done(((f32[1024,512]{1,0:T(8,128)}, f32[1024,512]{1,0:T(8,128)}, f32[1024,512]{1,0:T(8,128)}, f32[1024,512]{1,0:T(8,128)}), (f32[1024,512]{1,0:T(8,128)}, f32[1024,512]{1,0:T(8,128)}, f32[1024,512]{1,0:T(8,128)}, ...) | async-done | bytes 8388624 | tf_op jit(solution)/shard_map/psum | solution.py:11
  214.0 17.6 %negate_bitcast_fusion.1 = f32[1024,512]{1,0:T(8,128)} fusion(f32[1024,2048]{1,0:T(8,128)} %param.8, f32[1024,512]{1,0:T(8,128)} %get-tuple-element.8, f32[1024,512]{1,0:T(8,128)} %get-tuple-element.9), kind=kOutput, calls=%fused_computation.9 | convolution fusion | flops 12886474752 | bytes 14680064 | tf_op jit(solution)/shard_map/dot_general | solution.py:15
  231.7 0.0 reduce-scatter.3.cloned.1.call-update
  231.7 0.0 reduce-scatter.5.cloned.1.call-start
  231.8 17.7 %negate_bitcast_fusion = f32[1024,512]{1,0:T(8,128)} fusion(f32[1024,2048]{1,0:T(8,128)} %param.8, f32[1024,512]{1,0:T(8,128)} %get-tuple-element.10, f32[1024,512]{1,0:T(8,128)} %get-tuple-element.11), kind=kOutput, calls=%fused_computation.8 | convolution fusion | flops 12886474752 | bytes 14680064 | tf_op jit(solution)/shard_map/dot_general | solution.py:15
  249.4 0.0 reduce-scatter.5.cloned.1.call-update
  249.5 0.0 copy-start.2
  249.5 0.2 all-reduce.5.cloned.1.call-start
  249.7 3.1 fusion.17
  252.8 9.0 %reduce-scatter.3.cloned.1.call-done = f32[128,512]{1,0:T(8,128)} async-done(((f32[1024,512]{1,0:T(8,128)}), f32[128,512]{1,0:T(8,128)}) %reduce-scatter.3.cloned.1.call-update) | async-done | bytes 262160 | tf_op jit(solution)/shard_map/reduce_scatter | solution.py:33
  261.8 1.0 broadcast_multiply_fusion
  262.9 0.0 copy-start.6
  262.9 0.7 copy-done.6
  263.6 0.0 copy-done.2
  263.6 2.0 fusion.18
  265.6 31.1 %reduce-scatter.5.cloned.1.call-done = f32[128,512]{1,0:T(8,128)} async-done(((f32[1024,512]{1,0:T(8,128)}), f32[128,512]{1,0:T(8,128)}) %reduce-scatter.5.cloned.1.call-update) | async-done | bytes 262160 | tf_op jit(solution)/shard_map/reduce_scatter | solution.py:33
  296.7 0.0 copy-start.7
  296.7 0.0 copy-start.10
  296.7 2.5 add_multiply_fusion
  299.2 0.0 copy-start.9
  299.2 1.0 fusion.20
  300.3 0.0 copy-done.7
  300.3 0.0 copy-done.10
  300.3 2.0 fusion.16
  302.3 0.0 copy-done.9
  302.3 2.0 convolution_add_fusion.1
  304.3 0.0 all-reduce.5.cloned.1.call-update
  304.3 2.9 fusion.19
  307.2 152.7 %all-reduce.5.cloned.1.call-done = (f32[512,512]{1,0:T(8,128)}, f32[512,512]{1,0:T(8,128)}, f32[512,512]{1,0:T(8,128)}) async-done(((f32[512,512]{1,0:T(8,128)}, f32[512,512]{1,0:T(8,128)}, f32[512,512]{1,0:T(8,128)}), (f32[512,512]{1,0:T(8,128)}, f32[512,512]{1,0:T(8,128)}, f32[512,512]{1,0:T(8,128)})) %all-reduce.5.cloned.1.call-update) | async-done | bytes 3145744 | tf_op jit(solution)/shard_map/psum | solution.py:61
  459.8 0.0 copy-start.11
  459.8 3.2 convolution_subtract_fusion.1
  463.0 0.0 copy-start.5
  463.0 0.0 copy-done.11
  463.0 0.0 copy-start.3
  463.1 0.0 copy-start.8
  463.1 1.9 fusion.13
  464.9 0.0 copy-done.5
  464.9 0.0 copy-start.4
  465.0 0.0 copy-done.3
  465.0 0.0 copy-done.8
  465.0 2.9 fusion.12
  467.9 0.0 copy-done.4
  (3 shorter events, 0.0 us)
Async XLA Ops:
  7.2 1.2 copy-start
  7.2 4.4 copy-start.1
  7.2 32.5 %all-gather.5.cloned.1.call-start = ((), (), s32[]{:S(2)}) async-start(), calls=%async_computation.4 | async-start | bytes 2359296 | tf_op jit(solution)/shard_map/all_gather | solution.py:25
  10.8 56.7 %all-gather.3.cloned.1.call-start = ((), (), s32[]{:S(2)}) async-start(), calls=%async_computation.2 | async-start | bytes 2359296 | tf_op jit(solution)/shard_map/all_gather | solution.py:25
  14.0 200.0 %all-reduce.7.cloned.1.call-start = ((), (), s32[]{:S(2)}) async-start(), calls=%async_computation.7 | async-start | bytes 16777216 | tf_op jit(solution)/shard_map/psum | solution.py:11
  71.7 190.2 %reduce-scatter.3.cloned.1.call-start = ((), (), s32[]{:S(2)}) async-start(), calls=%async_computation.3 | async-start | bytes 2359296 | tf_op jit(solution)/shard_map/reduce_scatter | solution.py:33
  231.7 65.0 %reduce-scatter.5.cloned.1.call-start = ((), (), s32[]{:S(2)}) async-start(), calls=%async_computation.5 | async-start | bytes 2359296 | tf_op jit(solution)/shard_map/reduce_scatter | solution.py:33
  249.5 14.1 %copy-start.2 = (f32[128,512]{1,0:T(8,128)S(1)}, f32[128,512]{1,0:T(8,128)}, u32[]{:S(2)}) copy-start(f32[128,512]{1,0:T(8,128)} %convolution_multiply_fusion) | copy-start | bytes 786436
  249.5 210.4 %all-reduce.5.cloned.1.call-start = ((), (), s32[]{:S(2)}) async-start(), calls=%async_computation.6 | async-start | bytes 6291456 | tf_op jit(solution)/shard_map/psum | solution.py:61
  262.9 0.7 copy-start.6
  296.7 3.6 copy-start.7
  296.7 3.6 copy-start.10
  299.2 3.1 copy-start.9
  459.8 3.2 copy-start.11
  463.0 1.9 copy-start.5
  463.0 1.9 copy-start.3
  463.1 1.9 copy-start.8
  464.9 2.9 copy-start.4
Sparse Core Ops, SparseCore 0:
  10.9 28.7 all-gather.4
  42.0 25.4 all-gather.2
  71.8 142.2 all-reduce.6
  231.8 29.9 reduce-scatter.2
  264.2 32.4 reduce-scatter.4
  304.5 155.3 all-reduce.4
where the time goes:
time: 475 us
  waiting for transfers between devices  384 us (81%)
  matrix products  63.5 us (13%)
  between operations  14.3 us (3%)
  other arithmetic  11.1 us (2%)
    psum x1, waiting for transfers between devices, body(): diag_total = lax.psum(quad_one, ('row', 'col'))  153 us
    psum x1, waiting for transfers between devices, spread(): return lax.psum(jnp.where(mine, x, jnp.zeros_like(x)), axis)  142 us
    dot_general x14, matrix products, product(): jnp.dot(left, right, precision=lax.Precision.HIGHEST, preferred_element_t...  63.5 us
    all_gather x2, waiting for transfers between devices, panel_apart(): row_block = lax.all_gather(normal, 'col', axis=0, tiled=True)  49.2 us
    reduce_scatter x2, waiting for transfers between devices, sweep(): lax.psum_scatter(-product(trailing, col_block), 'col', scatter_dimension=...  40.2 us
  transfers between devices with their start and end apart: 6, of which 6 were waited for; matrix products, arithmetic and copies ran while one was open for 7% of the time, Pallas kernels for 0%

commit v1 on v0

--- a/solution.py
+++ b/solution.py
@@ -58,7 +58,7 @@
     rows_two, cols_two = panel_apart(normal_two, col_index, spread_count)
     summed_one, quad_one = sweep(trailing, cols_one, normal_one)
     column_one = mask_one * summed_one
-    diag_total = lax.psum(quad_one, ("row", "col"))
+    diag_total = lax.psum(lax.psum(quad_one, "row"), "col")
     diagonal_one = product(inverse_one.T, inverse_one) - diag_total
     normal_top = product(factor_two_top, inverse_two)
     summed_two, quad_two = sweep(trailing, cols_two, normal_two)

time: 475 us -> 613 us (1.29)
  waiting for transfers between devices: 384 us -> 521 us
    psum x1 -> x3, waiting for transfers between devices: 153 us -> 327 us  [the longest x2 173 us: body(): diag_total = lax.psum(lax.psum(quad_one, 'row'), 'col')]
    psum x1, waiting for transfers between devices: 142 us -> 101 us  [spread(): return lax.psum(jnp.where(mine, x, jnp.zeros_like(x)), axis)]
    reduce_scatter x2, waiting for transfers between devices: 40.2 us -> 53.9 us  [sweep(): lax.psum_scatter(-product(trailing, col_block), 'col', scatter_dimension=...]
    all_gather x2, waiting for transfers between devices: 49.2 us -> 38.9 us  [panel_apart(): row_block = lax.all_gather(normal, 'col', axis=0, tiled=True)]
  transfers between devices with their start and end apart: 6 -> 8, of which waited for: 6 -> 8; matrix products, arithmetic and copies ran while one was open for 7% -> 6% of each run, Pallas kernels for 0% -> 0%
where the time goes in v1:
time: 613 us; the launch traced here: 612 us
  waiting for transfers between devices  521 us (85%)
  matrix products  65 us (11%)
  between operations  14.3 us (2%)
  other arithmetic  9.62 us (2%)
    psum x2, waiting for transfers between devices, body(): diag_total = lax.psum(lax.psum(quad_one, 'row'), 'col')  173 us
    psum x1, waiting for transfers between devices, body(): lax.psum((product(column_one.T, normal_two), product(normal_two.T, local_...  154 us
    psum x1, waiting for transfers between devices, spread(): return lax.psum(jnp.where(mine, x, jnp.zeros_like(x)), axis)  101 us
    dot_general x14, matrix products, product(): jnp.dot(left, right, precision=lax.Precision.HIGHEST, preferred_element_t...  65 us
    reduce_scatter x2, waiting for transfers between devices, sweep(): lax.psum_scatter(-product(trailing, col_block), 'col', scatter_dimension=...  53.9 us
    all_gather x2, waiting for transfers between devices, panel_apart(): row_block = lax.all_gather(normal, 'col', axis=0, tiled=True)  38.9 us
  transfers between devices with their start and end apart: 8, of which 8 were waited for; matrix products, arithmetic and copies ran while one was open for 6% of the time, Pallas kernels for 0%

profile of v1, /device:TPU:1, one launch (start us, length us, event | category | flops | bytes accessed | tf_op | source)
XLA Modules:
  0.0 612.2 jit_solution(11268611719453303192)
XLA Ops:
  7.2 0.0 copy-start
  7.2 0.0 all-gather.3.cloned.1.call-start
  7.3 0.8 compare_reduce_fusion.1
  8.1 2.7 convolution_multiply_fusion.1
  10.8 0.0 all-gather.3.cloned.1.call-update
  10.8 0.0 all-reduce.14.cloned.1.call-start
  10.9 28.8 %all-gather.3.cloned.1.call-done = f32[1024,512]{1,0:T(8,128)} async-done(((f32[128,512]{1,0:T(8,128)}), f32[1024,512]{1,0:T(8,128)}) %all-gather.3.cloned.1.call-update) | async-done | bytes 2097168 | tf_op jit(solution)/shard_map/all_gather | solution.py:25
  39.8 4.4 broadcast_select_fusion.3
  44.1 0.0 copy-start.12
  44.1 0.0 copy-start.11
  44.1 0.0 all-reduce.14.cloned.1.call-update
  44.1 0.0 all-gather.5.cloned.1.call-start
  44.2 0.6 copy-done.12
  44.8 0.1 compare_reduce_fusion
  44.9 0.0 copy-done
  44.9 0.2 copy-done.11
  45.1 1.4 convolution_multiply_fusion
  46.5 0.0 all-gather.5.cloned.1.call-update
  46.5 0.0 reduce-scatter.3.cloned.1.call-start
  46.6 101.2 %all-reduce.14.cloned.1.call-done = (f32[1024,512]{1,0:T(8,128)}, f32[1024,512]{1,0:T(8,128)}) async-done(((f32[1024,512]{1,0:T(8,128)}, f32[1024,512]{1,0:T(8,128)}), (f32[1024,512]{1,0:T(8,128)}, f32[1024,512]{1,0:T(8,128)})) %all-reduce.14.cloned.1.call-update) | async-done | bytes 4194320 | tf_op jit(solution)/shard_map/psum | solution.py:11
  147.8 17.6 %negate_bitcast_fusion.1 = f32[1024,512]{1,0:T(8,128)} fusion(f32[1024,2048]{1,0:T(8,128)} %param.8, f32[1024,512]{1,0:T(8,128)} %get-tuple-element.10, f32[1024,512]{1,0:T(8,128)} %get-tuple-element.11), kind=kOutput, calls=%fused_computation.9 | convolution fusion | flops 12886474752 | bytes 14680064 | tf_op jit(solution)/shard_map/dot_general | solution.py:15
  165.4 0.0 reduce-scatter.3.cloned.1.call-update
  165.4 0.0 copy-start.6
  165.4 0.0 all-reduce.12.cloned.1.call-start
  165.5 10.1 %all-gather.5.cloned.1.call-done = f32[1024,512]{1,0:T(8,128)} async-done(((f32[128,512]{1,0:T(8,128)}), f32[1024,512]{1,0:T(8,128)}) %all-gather.5.cloned.1.call-update) | async-done | bytes 2097168 | tf_op jit(solution)/shard_map/all_gather | solution.py:25
  175.5 4.2 broadcast_select_fusion.1
  179.8 28.6 %reduce-scatter.3.cloned.1.call-done = f32[128,512]{1,0:T(8,128)} async-done(((f32[1024,512]{1,0:T(8,128)}), f32[128,512]{1,0:T(8,128)}) %reduce-scatter.3.cloned.1.call-update) | async-done | bytes 262160 | tf_op jit(solution)/shard_map/reduce_scatter | solution.py:33
  208.3 0.0 copy-done.6
  208.3 2.9 fusion.16
  211.3 0.0 all-reduce.12.cloned.1.call-update
  211.3 0.0 reduce-scatter.5.cloned.1.call-start
  211.4 116.4 %all-reduce.12.cloned.1.call-done = (f32[512,512]{1,0:T(8,128)}, f32[1024,512]{1,0:T(8,128)}, f32[1024,512]{1,0:T(8,128)}) async-done(((f32[512,512]{1,0:T(8,128)}, f32[1024,512]{1,0:T(8,128)}, f32[1024,512]{1,0:T(8,128)}), (f32[512,512]{1,0:T(8,128)}, f32[1024,512]{1,0:T(8,128)}, f32[1024,512]{1,0:T(8,128)})) %all-reduce.12.cloned.1.call-update) | async-done | bytes 5242896 | tf_op jit(solution)/shard_map/psum | solution.py:61
  327.7 17.6 %negate_bitcast_fusion = f32[1024,512]{1,0:T(8,128)} fusion(f32[1024,2048]{1,0:T(8,128)} %param.8, f32[1024,512]{1,0:T(8,128)} %get-tuple-element.8, f32[1024,512]{1,0:T(8,128)} %get-tuple-element.9), kind=kOutput, calls=%fused_computation.8 | convolution fusion | flops 12886474752 | bytes 14680064 | tf_op jit(solution)/shard_map/dot_general | solution.py:15
  345.4 0.0 reduce-scatter.5.cloned.1.call-update
  345.4 0.0 copy-start.2
  345.4 0.2 all-reduce.8.cloned.1.call-start
  345.6 1.0 copy-done.7
  346.6 1.8 fusion.17
  348.4 0.0 copy-done.10
  348.5 0.1 broadcast_multiply_fusion
  348.5 0.0 copy-done.2
  348.6 0.0 copy-start.5
  348.6 2.0 fusion.18
  350.6 0.0 all-reduce.8.cloned.1.call-update
  350.6 0.0 all-reduce.10.cloned.1.call-start
  350.6 25.3 %reduce-scatter.5.cloned.1.call-done = f32[128,512]{1,0:T(8,128)} async-done(((f32[1024,512]{1,0:T(8,128)}), f32[128,512]{1,0:T(8,128)}) %reduce-scatter.5.cloned.1.call-update) | async-done | bytes 262160 | tf_op jit(solution)/shard_map/reduce_scatter | solution.py:33
  375.9 2.4 add_multiply_fusion
  378.4 0.0 copy-done.5
  378.4 1.0 fusion.20
  379.4 0.0 copy-done.9
  379.4 2.0 convolution_add_fusion.1
  381.4 0.0 all-reduce.10.cloned.1.call-update
  381.5 0.0 copy-start.1
  381.5 2.8 fusion.19
  384.3 56.1 %all-reduce.8.cloned.1.call-done = f32[512,512]{1,0:T(8,128)} async-done(((f32[512,512]{1,0:T(8,128)}), f32[512,512]{1,0:T(8,128)}) %all-reduce.8.cloned.1.call-update) | async-done | bytes 1048592 | tf_op jit(solution)/shard_map/psum | solution.py:61
  440.4 0.0 copy-done.1
  440.4 4.1 convolution_subtract_fusion.1
  444.5 154.3 %all-reduce.10.cloned.1.call-done = (f32[512,512]{1,0:T(8,128)}, f32[512,512]{1,0:T(8,128)}) async-done(((f32[512,512]{1,0:T(8,128)}, f32[512,512]{1,0:T(8,128)}), (f32[512,512]{1,0:T(8,128)}, f32[512,512]{1,0:T(8,128)})) %all-reduce.10.cloned.1.call-update) | async-done | bytes 2097168 | tf_op jit(solution)/shard_map/psum | solution.py:67
  598.8 3.6 fusion.13
  602.4 0.0 copy-start.4
  602.4 0.0 copy-done.3
  602.4 0.0 copy-done.8
  602.4 2.9 fusion.12
  605.4 0.0 copy-done.4
  (8 shorter events, 0.0 us)
Async XLA Ops:
  7.2 37.7 %copy-start = (f32[512,512]{1,0:T(8,128)S(1)}, f32[512,512]{1,0:T(8,128)}, u32[]{:S(2)}) copy-start(f32[512,512]{1,0:T(8,128)} %param.13) | copy-start | bytes 3145732
  7.2 32.6 %all-gather.3.cloned.1.call-start = ((), (), s32[]{:S(2)}) async-start(), calls=%async_computation.2 | async-start | bytes 2359296 | tf_op jit(solution)/shard_map/all_gather | solution.py:25
  10.8 137.0 %all-reduce.14.cloned.1.call-start = ((), (), s32[]{:S(2)}) async-start(), calls=%async_computation.9 | async-start | bytes 8388608 | tf_op jit(solution)/shard_map/psum | solution.py:11
  44.1 0.7 copy-start.12
  44.1 1.0 copy-start.11
  44.1 131.4 %all-gather.5.cloned.1.call-start = ((), (), s32[]{:S(2)}) async-start(), calls=%async_computation.5 | async-start | bytes 2359296 | tf_op jit(solution)/shard_map/all_gather | solution.py:25
  46.5 161.8 %reduce-scatter.3.cloned.1.call-start = ((), (), s32[]{:S(2)}) async-start(), calls=%async_computation.3 | async-start | bytes 2359296 | tf_op jit(solution)/shard_map/reduce_scatter | solution.py:33
  165.4 42.9 %copy-start.6 = (f32[128,512]{1,0:T(8,128)S(1)}, f32[128,512]{1,0:T(8,128)}, u32[]{:S(2)}) copy-start(f32[128,512]{1,0:T(8,128)} %convolution_multiply_fusion.1) | copy-start | bytes 786436
  165.4 162.3 %all-reduce.12.cloned.1.call-start = ((), (), s32[]{:S(2)}) async-start(), calls=%async_computation.8 | async-start | bytes 10485760 | tf_op jit(solution)/shard_map/psum | solution.py:61
  211.3 164.6 %reduce-scatter.5.cloned.1.call-start = ((), (), s32[]{:S(2)}) async-start(), calls=%async_computation.6 | async-start | bytes 2359296 | tf_op jit(solution)/shard_map/reduce_scatter | solution.py:33
  345.4 1.2 copy-start.7
  345.4 3.2 copy-start.2
  345.4 95.0 %all-reduce.8.cloned.1.call-start = ((), (), s32[]{:S(2)}) async-start(), calls=%async_computation.4 | async-start | bytes 2097152 | tf_op jit(solution)/shard_map/psum | solution.py:61
  346.6 1.9 copy-start.10
  348.6 29.8 %copy-start.5 = (f32[128,512]{1,0:T(8,128)}, f32[128,512]{1,0:T(8,128)S(1)}, u32[]{:S(2)}) copy-start(f32[128,512]{1,0:T(8,128)S(1)} %broadcast_multiply_fusion) | copy-start | bytes 786436
  350.6 248.2 %all-reduce.10.cloned.1.call-start = ((), (), s32[]{:S(2)}) async-start(), calls=%async_computation.7 | async-start | bytes 4194304 | tf_op jit(solution)/shard_map/psum | solution.py:67
  375.9 3.5 copy-start.9
  381.5 59.0 %copy-start.1 = (f32[512,512]{1,0:T(8,128)S(1)}, f32[512,512]{1,0:T(8,128)}, u32[]{:S(2)}) copy-start(f32[512,512]{1,0:T(8,128)} %param.10) | copy-start | bytes 3145732
  598.8 3.6 copy-start.3
  598.8 3.6 copy-start.8
  602.4 3.0 copy-start.4
Sparse Core Ops, SparseCore 0:
  11.0 28.7 all-gather.2
  44.3 103.4 all-reduce.13
  150.1 25.3 all-gather.4
  177.8 30.4 reduce-scatter.2
  212.5 115.1 all-reduce.11
  345.5 30.3 reduce-scatter.4
  378.4 62.0 all-reduce.7
  446.9 151.8 all-reduce.9
